TPU v7x, 512 devices: a whole 4x8x8 slice. The times are simulated.
512 devices in a mesh: context: 32 (over y, x), tensor: 16 (over z, core).
Axes of the slice: x: 4, y: 8, z: 8, core: 2. Of those that a mesh axis runs over, the one named last changes fastest.
Arguments:
- queries: bfloat16 [1, 16384, 4096], P(None, 'context', 'tensor'), may hold values from -6 to 6
- keys: bfloat16 [1, 16384, 4096], P(None, 'context', 'tensor'), may hold values from -0.546875 to 0.546875
- spike_counts: int32 [1, 16384, 4096], P(None, 'context', 'tensor'), may hold values from -4 to 4
- spike_scale: float32 [4096], P('tensor'), may hold values from 0.5 to 2
- log_decay: float32 [1, 32, 16384], P(None, 'tensor', 'context'), may hold values from -3 to 0, as said below
- norm_gain: float32 [4096], P('tensor'), may hold values from 0.5 to 1.5
- out_weight: bfloat16 [4096, 8192], P('context', 'tensor'), may hold values from -0.09375 to 0.09375
- residual_in: bfloat16 [1, 16384, 8192], P(None, 'context', 'tensor'), may hold values from -6 to 6
Outputs:
- residual_out: bfloat16 [1, 16384, 8192], P(None, 'context', 'tensor')
Inputs may be any that keep to these rules, and one draw needn't show every extreme that they name: log_decay is negative.
All inputs are finite; a program needn't handle non-finite values.
Results may differ from a plain program's by a relative error of at most 0.0095.
Values may be sent and summed in bfloat16 or wider, within the bound.
A program may use at most 64 MiB of HBM per device.

v0:
```python
import jax
import jax.numpy as jnp
from jax import lax
from jax.sharding import PartitionSpec as P

epsilon = 1e-06


def prefix_2(value, axis, combine, identity):
    size, position = (lax.axis_size(axis), lax.axis_index(axis))
    everything = jax.tree.map(
        lambda part, kind: lax.all_gather(part.astype(kind), axis),
        value,
        (jnp.bfloat16, jnp.bfloat16),
    )
    start = jax.tree.map(
        lambda part, zero: jnp.broadcast_to(jnp.asarray(zero, part.dtype), part.shape),
        value,
        identity,
    )

    def lap(k, before):
        reached = k < position
        new = combine(
            before, jax.tree.map(lambda part, own: part[k].astype(own.dtype), everything, value)
        )
        return jax.tree.map(lambda a, b: jnp.where(reached, a, b), new, before)

    return lax.fori_loop(0, size, lap, start)


def combine(earlier, later):
    return (earlier[0] * later[0], later[0][..., None, None] * earlier[1] + later[1])


def local(queries, keys, spike_counts, spike_scale, log_decay, norm_gain, out_weight, residual_in):
    requests, block, width_here = queries.shape
    heads = log_decay.shape[1]
    head_size = width_here // heads
    values = (spike_counts.astype(jnp.float32) * spike_scale).astype(jnp.bfloat16)

    def split_heads(array):
        return array.reshape(requests, block, heads, head_size).transpose(0, 2, 1, 3)

    query_h = split_heads(queries)
    key_h = split_heads(keys)
    value_h = split_heads(values)
    cumulative = jnp.cumsum(log_decay, axis=2)
    vocabulary_identifiers = jnp.arange(block)
    causal = vocabulary_identifiers[:, None] >= vocabulary_identifiers[None, :]
    gaps = cumulative[..., :, None] - cumulative[..., None, :]
    decay_mat = jnp.exp(jnp.where(causal, gaps, -1e30))
    scores = jnp.einsum("rhtd,rhsd->rhts", query_h, key_h, preferred_element_type=jnp.float32)
    weights = (scores * decay_mat).astype(jnp.bfloat16)
    intra = jnp.einsum("rhts,rhsd->rhtd", weights, value_h, preferred_element_type=jnp.float32)
    to_end = jnp.exp(cumulative[..., -1:] - cumulative)
    weighted_keys = (key_h.astype(jnp.float32) * to_end[..., None]).astype(jnp.bfloat16)
    own_state = jnp.einsum(
        "rhsd,rhse->rhde", weighted_keys, value_h, preferred_element_type=jnp.float32
    )
    span_decay = jnp.exp(cumulative[..., -1])
    prefix = prefix_2(
        (span_decay, own_state),
        "context",
        combine,
        (jnp.ones_like(span_decay), jnp.zeros_like(own_state)),
    )
    incoming = prefix[1]
    carried = jnp.exp(cumulative)[..., None] * jnp.einsum(
        "rhtd,rhde->rhte", query_h.astype(jnp.float32), incoming, precision=lax.Precision.HIGHEST
    )
    mixed = intra + carried
    scale = lax.rsqrt(jnp.mean(mixed * mixed, axis=-1, keepdims=True) + epsilon)
    normed = (mixed * scale * norm_gain.reshape(1, heads, 1, head_size)).astype(jnp.bfloat16)
    normed = normed.transpose(0, 2, 1, 3).reshape(requests * block, width_here)
    all_heads = lax.all_gather(normed, "tensor", axis=1, tiled=True)
    projected = jnp.dot(
        all_heads,
        lax.all_gather(out_weight, "context", axis=0, tiled=True),
        preferred_element_type=jnp.float32,
    )
    projected = projected.reshape(requests, block, out_weight.shape[1])
    return (residual_in.astype(jnp.float32) + projected).astype(jnp.bfloat16)


def solution(mesh):
    in_specs = (
        P(None, "context", "tensor"),
        P(None, "context", "tensor"),
        P(None, "context", "tensor"),
        P("tensor"),
        P(None, "tensor", "context"),
        P("tensor"),
        P("context", "tensor"),
        P(None, "context", "tensor"),
    )
    out_specs = P(None, "context", "tensor")
    return jax.shard_map(local, mesh=mesh, in_specs=in_specs, out_specs=out_specs, check_vma=False)
```

profile of v0, /device:TPU:1, one launch (start us, length us, event | category | flops | bytes accessed | tf_op | source)
XLA Modules:
  0.0 247.4 jit_solution(11480079209673487597)
XLA Ops:
  8.4 1.1 copy.44
  9.5 1.1 multiply_convert_fusion.3
  12.7 31.4 %all-gather = bf16[32,2,1]{2,1,0:T(2,128)(2,1)S(1)} all-gather(bf16[1,2,1]{2,1,0:T(2,128)(2,1)S(1)} %get-tuple-element.154), channel_id=2, replica_groups=mesh['context'=32,'tensor'=16] {'context'}, dimensions={0}, use_global_device_ids=true | all-gather | bytes 132 | tf_op jit(solution)/shard_map/all_gather | solution.py:12
  44.3 52.7 %all-gather.10.cloned.1.call-done = bf16[64,128,128]{2,1,0:T(8,128)(2,1)} async-done(((bf16[2,128,128]{2,1,0:T(8,128)(2,1)}), bf16[64,128,128]{2,1,0:T(8,128)(2,1)}) %all-gather.10.cloned.1.call-update) | async-done | bytes 2097168 | tf_op jit(solution)/shard_map/all_gather | solution.py:12
  97.0 36.8 %while.14 = (s32[]{:T(128)}, f32[1,2,128,128]{3,2,1,0:T(8,128)S(1)}, s32[]{:T(128)}, bf16[32,1,2]{0,2,1:T(2,128)(2,1)S(1)}, bf16[32,1,2,128,128]{4,3,2,1,0:T(8,128)(2,1)}, /*index=5*/s32[]{:T(128)}, s32[]{:T(128)}) while((s32[]{:T(128)}, f32[1,2,128,128]{3,2,1,0:T(8,128)S(1)}, s32[]{:T(128)}, bf16[32,1,2]{0,2,1:T(2,128)(2,1)S(1)}, ...), condition=%wide.region_3.4_spmd.clone, body=%wide.region_2.3_spmd.clone.sunk | while | flops 163846 | bytes 327829 | solution.py:29
  98.3 0.9 fusion.25
  99.5 0.9 fusion.25
  102.9 0.9 fusion.25
  105.2 0.9 fusion.25
  108.7 0.9 fusion.25
  112.1 0.9 fusion.25
  114.4 0.9 fusion.25
  115.6 0.9 fusion.25
  116.7 0.9 fusion.25
  119.0 0.9 fusion.25
  121.3 0.9 fusion.25
  122.5 0.9 fusion.25
  124.8 0.9 fusion.25
  128.2 0.9 fusion.25
  130.5 0.9 fusion.25
  134.2 1.0 multiply_reduce_fusion
  136.1 49.7 %all-gather.8.cloned.1.call-done = bf16[4096,512]{1,0:T(8,128)(2,1)} async-done(((bf16[128,512]{1,0:T(8,128)(2,1)}), bf16[4096,512]{1,0:T(8,128)(2,1)}) %all-gather.8.cloned.1.call-update) | async-done | bytes 4194320 | tf_op jit(solution)/shard_map/all_gather | solution.py:79
  185.8 48.4 %all-gather.6.cloned.1.call-done = bf16[512,4096]{0,1:T(8,128)(2,1)} async-done(((bf16[512,256]{0,1:T(8,128)(2,1)}), bf16[512,4096]{0,1:T(8,128)(2,1)}) %all-gather.6.cloned.1.call-update) | async-done | bytes 4194320 | tf_op jit(solution)/shard_map/all_gather | solution.py:76
  234.3 6.6 %fusion.3 = bf16[1,512,512]{2,1,0:T(8,128)(2,1)} fusion(bf16[512,4096]{0,1:T(8,128)(2,1)} %all-gather.6.cloned.1.call-done, bf16[4096,512]{1,0:T(8,128)(2,1)} %all-gather.8.cloned.1.call-done, bf16[1,512,512]{2,1,0:T(8,128)(2,1)S(1)} %copy-done.2), kind=kOutput, calls=%fused_computation.8 | convolution fusion | flops 2148270080 | bytes 9437184 | tf_op jit(solution)/shard_map/dot_general | solution.py:77
  (148 shorter events, 27.3 us)
Async XLA Ops:
  6.5 37.7 %copy-start = (bf16[1,512,256]{2,1,0:T(8,128)(2,1)S(1)}, bf16[1,512,256]{2,1,0:T(8,128)(2,1)}, u32[]{:S(2)}) copy-start(bf16[1,512,256]{2,1,0:T(8,128)(2,1)} %param.10) | copy-start | bytes 786436
  6.5 90.4 %all-gather.10.cloned.1.call-start = ((), (), s32[]{:S(2)}) async-start(), calls=%async_computation.2 | async-start | bytes 2162688 | tf_op jit(solution)/shard_map/all_gather | solution.py:12
  11.8 174.0 %all-gather.8.cloned.1.call-start = ((), (), s32[]{:S(2)}) async-start(), calls=%async_computation.1 | async-start | bytes 4325376 | tf_op jit(solution)/shard_map/all_gather | solution.py:79
  12.6 221.7 %all-gather.6.cloned.1.call-start = ((), (), s32[]{:S(2)}) async-start(), calls=%async_computation | async-start | bytes 4456448 | tf_op jit(solution)/shard_map/all_gather | solution.py:76
  134.2 1.1 copy-start.1
  134.2 100.1 %copy-start.2 = (bf16[1,512,512]{2,1,0:T(8,128)(2,1)S(1)}, bf16[1,512,512]{2,1,0:T(8,128)(2,1)}, u32[]{:S(2)}) copy-start(bf16[1,512,512]{2,1,0:T(8,128)(2,1)} %param.17) | copy-start | bytes 1572868
Sparse Core Ops, SparseCore 0:
  11.9 85.0 all-gather.9
  100.1 85.6 all-gather.7
  187.9 46.2 all-gather.5
where the time goes:
time: 249 us; the launch traced here: 247 us
  waiting for transfers between devices  152 us (61%)
  other arithmetic  33 us (13%)
  blocking collectives  31.4 us (13%)
  between operations  13.2 us (5%)
  matrix products  8.93 us (4%)
  local copies, waits for them, and re-layouts  8.36 us (3%)
    all_gather x1, waiting for transfers between devices, prefix_2(): lax.all_gather(part.astype(kind), axis)  52.7 us
    all_gather x1, waiting for transfers between devices, local(): lax.all_gather(out_weight, 'context', axis=0, tiled=True)  49.7 us
    all_gather x1, waiting for transfers between devices, local(): all_heads = lax.all_gather(normed, 'tensor', axis=1, tiled=True)  48.4 us
    all_gather x1, blocking collectives, prefix_2(): lax.all_gather(part.astype(kind), axis)  31.4 us
    select_n x32, other arithmetic, lap(): return jax.tree.map(lambda a, b: jnp.where(reached, a, b), new, before)  29.7 us
    dot_general x1, matrix products, local(): jnp.dot(all_heads, lax.all_gather(out_weight, 'context', axis=0, tiled=Tr...  6.61 us
    dynamic_slice x64, local copies, waits for them, and re-layouts, lap(): part[k].astype(own.dtype)  6.03 us
  transfers between devices with their start and end apart: 3, of which 3 were waited for; matrix products, arithmetic and copies ran while one was open for 16% of the time, Pallas kernels for 0%

commit v1 on v0

--- a/solution.py
+++ b/solution.py
@@ -4,6 +4,19 @@
 from jax.sharding import PartitionSpec as P
 
 epsilon = 1e-06
+
+
+def gather_around(shard, axis, dim):
+    ways = lax.axis_size(axis)
+    up = [(d, (d + 1) % ways) for d in range(ways)]
+    down = [(d, (d - 1) % ways) for d in range(ways)]
+    earlier, later = ([shard], [shard])
+    for _ in range(ways // 2):
+        earlier.append(lax.ppermute(earlier[-1], axis, up))
+    for _ in range((ways - 1) // 2):
+        later.append(lax.ppermute(later[-1], axis, down))
+    line = jnp.concatenate([*earlier[::-1], *later[1:]], axis=dim)
+    return jnp.roll(line, (lax.axis_index(axis) - ways // 2) * shard.shape[dim], axis=dim)
 
 
 def prefix_2(value, axis, combine, identity):
@@ -73,7 +86,7 @@
     scale = lax.rsqrt(jnp.mean(mixed * mixed, axis=-1, keepdims=True) + epsilon)
     normed = (mixed * scale * norm_gain.reshape(1, heads, 1, head_size)).astype(jnp.bfloat16)
     normed = normed.transpose(0, 2, 1, 3).reshape(requests * block, width_here)
-    all_heads = lax.all_gather(normed, "tensor", axis=1, tiled=True)
+    all_heads = gather_around(normed, "tensor", 1)
     projected = jnp.dot(
         all_heads,
         lax.all_gather(out_weight, "context", axis=0, tiled=True),

time: 249 us -> 236 us (0.948)
  the two profiles are of different devices: /device:TPU:1 before, /device:TPU:16 now
where the time goes in v1:
time: 236 us; the launch traced here: 234 us
  waiting for transfers between devices  84.8 us (36%)
  local copies, waits for them, and re-layouts  36.2 us (15%)
  blocking collectives  35.8 us (15%)
  other arithmetic  32.3 us (14%)
  starting transfers between devices  22 us (9%)
  between operations  13.5 us (6%)
  matrix products  8.97 us (4%)
    all_gather x1, waiting for transfers between devices, prefix_2(): lax.all_gather(part.astype(kind), axis)  49.7 us
    all_gather x1, blocking collectives, prefix_2(): lax.all_gather(part.astype(kind), axis)  35.8 us
    ppermute x8, waiting for transfers between devices, gather_around(): earlier.append(lax.ppermute(earlier[-1], axis, up))  33.1 us
    select_n x32, other arithmetic, lap(): return jax.tree.map(lambda a, b: jnp.where(reached, a, b), new, before)  29.7 us
    unnamed x34, local copies, waits for them, and re-layouts  26.2 us
    ppermute x7, starting transfers between devices, gather_around(): later.append(lax.ppermute(later[-1], axis, down))  22 us
    dot_general x1, matrix products, local(): jnp.dot(all_heads, lax.all_gather(out_weight, 'context', axis=0, tiled=Tr...  6.64 us
    dynamic_slice x64, local copies, waits for them, and re-layouts, lap(): part[k].astype(own.dtype)  6.03 us
  transfers between devices with their start and end apart: 17, of which 12 were waited for; matrix products, arithmetic and copies ran while one was open for 28% of the time, Pallas kernels for 0%

profile of v1, /device:TPU:16, one launch (start us, length us, event | category | flops | bytes accessed | tf_op | source)
XLA Modules:
  0.0 234.2 jit_solution(13460801782328462261)
XLA Ops:
  8.4 1.1 multiply_convert_fusion.3
  12.6 35.8 %all-gather = bf16[32,2,1]{2,1,0:T(2,128)(2,1)S(1)} all-gather(bf16[1,2,1]{2,1,0:T(2,128)(2,1)S(1)} %get-tuple-element.154), channel_id=2, replica_groups=mesh['context'=32,'tensor'=16] {'context'}, dimensions={0}, use_global_device_ids=true | all-gather | bytes 132 | tf_op jit(solution)/shard_map/all_gather | solution.py:25
  49.5 49.7 %all-gather.7.cloned.1.call-done = bf16[64,128,128]{2,1,0:T(8,128)(2,1)} async-done(((bf16[2,128,128]{2,1,0:T(8,128)(2,1)}), bf16[64,128,128]{2,1,0:T(8,128)(2,1)}) %all-gather.7.cloned.1.call-update) | async-done | bytes 2097168 | tf_op jit(solution)/shard_map/all_gather | solution.py:25
  99.2 36.5 %while.14 = (s32[]{:T(128)}, f32[1,2,128,128]{3,2,1,0:T(8,128)S(1)}, s32[]{:T(128)}, bf16[32,1,2]{0,2,1:T(2,128)(2,1)S(1)}, bf16[32,1,2,128,128]{4,3,2,1,0:T(8,128)(2,1)}, /*index=5*/s32[]{:T(128)}, s32[]{:T(128)}) while((s32[]{:T(128)}, f32[1,2,128,128]{3,2,1,0:T(8,128)S(1)}, s32[]{:T(128)}, bf16[32,1,2]{0,2,1:T(2,128)(2,1)S(1)}, ...), condition=%wide.region_3.4_spmd.clone, body=%wide.region_2.3_spmd.clone.sunk | while | flops 163846 | bytes 327821 | solution.py:42
  137.4 7.0 %collective-permute-done = bf16[512,256]{0,1:T(8,128)(2,1)S(1)} collective-permute-done((bf16[512,256]{0,1:T(8,128)(2,1)S(1)}, bf16[512,256]{0,1:T(8,128)(2,1)S(1)}, u32[]{:S(2)}, u32[]{:S(2)}) %collective-permute-start) | collective-permute-done | bytes 262176 | tf_op jit(solution)/shard_map/ppermute | solution.py:15
  144.4 3.0 %collective-permute-start.8 = (bf16[512,256]{0,1:T(8,128)(2,1)S(1)}, bf16[512,256]{0,1:T(8,128)(2,1)S(1)}, u32[]{:S(2)}, u32[]{:S(2)}) collective-permute-start(bf16[512,256]{0,1:T(8,128)(2,1)S(1)} %bitcast.59), channel_id=1, source_target_pairs={{0,15},{1,0},{2,1},{3,2},{4,3},{5,4},{6,5},{7,6},{8,7},{9,8},{10,9... | collective-permute-start | bytes 786440 | tf_op jit(solution)/shard_map/ppermute | solution.py:17
  147.3 4.1 %collective-permute-done.1 = bf16[512,256]{0,1:T(8,128)(2,1)S(1)} collective-permute-done((bf16[512,256]{0,1:T(8,128)(2,1)S(1)}, bf16[512,256]{0,1:T(8,128)(2,1)S(1)}, u32[]{:S(2)}, u32[]{:S(2)}) %collective-permute-start.1) | collective-permute-done | bytes 262176 | tf_op jit(solution)/shard_map/ppermute | solution.py:15
  151.4 3.0 %collective-permute-start.9 = (bf16[512,256]{0,1:T(8,128)(2,1)S(1)}, bf16[512,256]{0,1:T(8,128)(2,1)S(1)}, u32[]{:S(2)}, u32[]{:S(2)}) collective-permute-start(bf16[512,256]{0,1:T(8,128)(2,1)S(1)} %collective-permute-done.8), channel_id=1, source_target_pairs={{0,15},{1,0},{2,1},{3,2},{4,3},{5,4},{6,5},{7,6},{8,7},{9,8},{10,9... | collective-permute-start | bytes 786440 | tf_op jit(solution)/shard_map/ppermute | solution.py:17
  154.3 4.0 %collective-permute-done.2 = bf16[512,256]{0,1:T(8,128)(2,1)S(1)} collective-permute-done((bf16[512,256]{0,1:T(8,128)(2,1)S(1)}, bf16[512,256]{0,1:T(8,128)(2,1)S(1)}, u32[]{:S(2)}, u32[]{:S(2)}) %collective-permute-start.2) | collective-permute-done | bytes 262176 | tf_op jit(solution)/shard_map/ppermute | solution.py:15
  158.4 3.0 %collective-permute-start.10 = (bf16[512,256]{0,1:T(8,128)(2,1)S(1)}, bf16[512,256]{0,1:T(8,128)(2,1)S(1)}, u32[]{:S(2)}, u32[]{:S(2)}) collective-permute-start(bf16[512,256]{0,1:T(8,128)(2,1)S(1)} %collective-permute-done.9), channel_id=1, source_target_pairs={{0,15},{1,0},{2,1},{3,2},{4,3},{5,4},{6,5},{7,6},{8,7},{9,8},{10,9... | collective-permute-start | bytes 786440 | tf_op jit(solution)/shard_map/ppermute | solution.py:17
  161.3 4.0 %collective-permute-done.3 = bf16[512,256]{0,1:T(8,128)(2,1)S(1)} collective-permute-done((bf16[512,256]{0,1:T(8,128)(2,1)S(1)}, bf16[512,256]{0,1:T(8,128)(2,1)S(1)}, u32[]{:S(2)}, u32[]{:S(2)}) %collective-permute-start.3) | collective-permute-done | bytes 262176 | tf_op jit(solution)/shard_map/ppermute | solution.py:15
  165.4 3.4 %collective-permute-start.11 = (bf16[512,256]{0,1:T(8,128)(2,1)S(1)}, bf16[512,256]{0,1:T(8,128)(2,1)S(1)}, u32[]{:S(2)}, u32[]{:S(2)}) collective-permute-start(bf16[512,256]{0,1:T(8,128)(2,1)S(1)} %collective-permute-done.10), channel_id=1, source_target_pairs={{0,15},{1,0},{2,1},{3,2},{4,3},{5,4},{6,5},{7,6},{8,7},{9,8},{10,9... | collective-permute-start | bytes 786440 | tf_op jit(solution)/shard_map/ppermute | solution.py:17
  168.7 3.6 %collective-permute-done.4 = bf16[512,256]{0,1:T(8,128)(2,1)S(1)} collective-permute-done((bf16[512,256]{0,1:T(8,128)(2,1)S(1)}, bf16[512,256]{0,1:T(8,128)(2,1)S(1)}, u32[]{:S(2)}, u32[]{:S(2)}) %collective-permute-start.4) | collective-permute-done | bytes 262176 | tf_op jit(solution)/shard_map/ppermute | solution.py:15
  172.6 3.5 %collective-permute-start.12 = (bf16[512,256]{0,1:T(8,128)(2,1)S(1)}, bf16[512,256]{0,1:T(8,128)(2,1)S(1)}, u32[]{:S(2)}, u32[]{:S(2)}) collective-permute-start(bf16[512,256]{0,1:T(8,128)(2,1)S(1)} %collective-permute-done.11), channel_id=1, source_target_pairs={{0,15},{1,0},{2,1},{3,2},{4,3},{5,4},{6,5},{7,6},{8,7},{9,8},{10,9... | collective-permute-start | bytes 786440 | tf_op jit(solution)/shard_map/ppermute | solution.py:17
  176.2 3.2 %collective-permute-done.5 = bf16[512,256]{0,1:T(8,128)(2,1)S(1)} collective-permute-done((bf16[512,256]{0,1:T(8,128)(2,1)S(1)}, bf16[512,256]{0,1:T(8,128)(2,1)S(1)}, u32[]{:S(2)}, u32[]{:S(2)}) %collective-permute-start.5) | collective-permute-done | bytes 262176 | tf_op jit(solution)/shard_map/ppermute | solution.py:15
  180.0 3.1 %collective-permute-start.13 = (bf16[512,256]{0,1:T(8,128)(2,1)S(1)}, bf16[512,256]{0,1:T(8,128)(2,1)S(1)}, u32[]{:S(2)}, u32[]{:S(2)}) collective-permute-start(bf16[512,256]{0,1:T(8,128)(2,1)S(1)} %collective-permute-done.12), channel_id=1, source_target_pairs={{0,15},{1,0},{2,1},{3,2},{4,3},{5,4},{6,5},{7,6},{8,7},{9,8},{10,9... | collective-permute-start | bytes 786440 | tf_op jit(solution)/shard_map/ppermute | solution.py:17
  183.2 3.4 %collective-permute-done.6 = bf16[512,256]{0,1:T(8,128)(2,1)} collective-permute-done((bf16[512,256]{0,1:T(8,128)(2,1)S(1)}, bf16[512,256]{0,1:T(8,128)(2,1)}, u32[]{:S(2)}, u32[]{:S(2)}) %collective-permute-start.6) | collective-permute-done | bytes 262176 | tf_op jit(solution)/shard_map/ppermute | solution.py:15
  187.0 3.1 %collective-permute-start.14 = (bf16[512,256]{0,1:T(8,128)(2,1)S(1)}, bf16[512,256]{0,1:T(8,128)(2,1)S(1)}, u32[]{:S(2)}, u32[]{:S(2)}) collective-permute-start(bf16[512,256]{0,1:T(8,128)(2,1)S(1)} %collective-permute-done.13), channel_id=1, source_target_pairs={{0,15},{1,0},{2,1},{3,2},{4,3},{5,4},{6,5},{7,6},{8,7},{9,8},{10,9... | collective-permute-start | bytes 786440 | tf_op jit(solution)/shard_map/ppermute | solution.py:17
  190.2 3.7 %collective-permute-done.7 = bf16[512,256]{0,1:T(8,128)(2,1)} collective-permute-done((bf16[512,256]{0,1:T(8,128)(2,1)}, bf16[512,256]{0,1:T(8,128)(2,1)}, u32[]{:S(2)}, u32[]{:S(2)}) %collective-permute-start.7) | collective-permute-done | bytes 262176 | tf_op jit(solution)/shard_map/ppermute | solution.py:15
  193.8 1.7 constant_dynamic-update-slice_fusion.31
  195.5 1.7 constant_dynamic-update-slice_fusion.30
  207.3 1.7 constant_dynamic-update-slice_fusion.15
  209.0 1.7 constant_dynamic-update-slice_fusion.14
  220.7 6.6 %fusion.10 = bf16[1,512,512]{2,1,0:T(8,128)(2,1)} fusion(bf16[4096,512]{1,0:T(8,128)(2,1)} %all-gather.5.cloned.1.call-done, bf16[512,8192]{0,1:T(8,128)(2,1)} %constant_dynamic-update-slice_fusion, s32[]{:T(128)S(6)} %select_n.42, bf16[1,512,512]{2,1,0:T(8,128)(2,1)} %param.17), kind=kOutput, calls=%fused_computation.10 | convolution fusion | flops 2148270080 | bytes 9437188 | tf_op jit(solution)/shard_map/dot_general | solution.py:90
  (203 shorter events, 65.2 us)
Async XLA Ops:
  6.5 130.7 %copy-start = (f32[256]{0:T(256)S(1)}, f32[256]{0:T(256)}, u32[]{:S(2)}) copy-start(f32[256]{0:T(256)} %param.15) | copy-start | bytes 3076
  6.5 92.7 %all-gather.7.cloned.1.call-start = ((), (), s32[]{:S(2)}) async-start(), calls=%async_computation.1 | async-start | bytes 2162688 | tf_op jit(solution)/shard_map/all_gather | solution.py:25
  11.8 209.0 %all-gather.5.cloned.1.call-start = ((), (), s32[]{:S(2)}) async-start(), calls=%async_computation | async-start | bytes 4325376 | tf_op jit(solution)/shard_map/all_gather | solution.py:92
  137.3 7.0 %collective-permute-start = (bf16[512,256]{0,1:T(8,128)(2,1)S(1)}, bf16[512,256]{0,1:T(8,128)(2,1)S(1)}, u32[]{:S(2)}, u32[]{:S(2)}) collective-permute-start(bf16[512,256]{0,1:T(8,128)(2,1)S(1)} %bitcast.58), channel_id=1, source_target_pairs={{0,1},{1,2},{2,3},{3,4},{4,5},{5,6},{6,7},{7,8},{8,9},{9,10},{10,1... | collective-permute-start | bytes 786440 | tf_op jit(solution)/shard_map/ppermute | solution.py:15
  144.4 7.0 %collective-permute-start.1 = (bf16[512,256]{0,1:T(8,128)(2,1)S(1)}, bf16[512,256]{0,1:T(8,128)(2,1)S(1)}, u32[]{:S(2)}, u32[]{:S(2)}) collective-permute-start(bf16[512,256]{0,1:T(8,128)(2,1)S(1)} %collective-permute-done), channel_id=1, source_target_pairs={{0,1},{1,2},{2,3},{3,4},{4,5},{5,6},{6,7},{7,8},{8,9},{9,10},{10,1... | collective-permute-start | bytes 786440 | tf_op jit(solution)/shard_map/ppermute | solution.py:15
  144.4 7.0 %collective-permute-start.8 = (bf16[512,256]{0,1:T(8,128)(2,1)S(1)}, bf16[512,256]{0,1:T(8,128)(2,1)S(1)}, u32[]{:S(2)}, u32[]{:S(2)}) collective-permute-start(bf16[512,256]{0,1:T(8,128)(2,1)S(1)} %bitcast.59), channel_id=1, source_target_pairs={{0,15},{1,0},{2,1},{3,2},{4,3},{5,4},{6,5},{7,6},{8,7},{9,8},{10,9... | collective-permute-start | bytes 786440 | tf_op jit(solution)/shard_map/ppermute | solution.py:17
  151.4 7.0 %collective-permute-start.2 = (bf16[512,256]{0,1:T(8,128)(2,1)S(1)}, bf16[512,256]{0,1:T(8,128)(2,1)S(1)}, u32[]{:S(2)}, u32[]{:S(2)}) collective-permute-start(bf16[512,256]{0,1:T(8,128)(2,1)S(1)} %collective-permute-done.1), channel_id=1, source_target_pairs={{0,1},{1,2},{2,3},{3,4},{4,5},{5,6},{6,7},{7,8},{8,9},{9,10},{10,1... | collective-permute-start | bytes 786440 | tf_op jit(solution)/shard_map/ppermute | solution.py:15
  151.4 7.0 %collective-permute-start.9 = (bf16[512,256]{0,1:T(8,128)(2,1)S(1)}, bf16[512,256]{0,1:T(8,128)(2,1)S(1)}, u32[]{:S(2)}, u32[]{:S(2)}) collective-permute-start(bf16[512,256]{0,1:T(8,128)(2,1)S(1)} %collective-permute-done.8), channel_id=1, source_target_pairs={{0,15},{1,0},{2,1},{3,2},{4,3},{5,4},{6,5},{7,6},{8,7},{9,8},{10,9... | collective-permute-start | bytes 786440 | tf_op jit(solution)/shard_map/ppermute | solution.py:17
  158.4 7.0 %collective-permute-start.3 = (bf16[512,256]{0,1:T(8,128)(2,1)S(1)}, bf16[512,256]{0,1:T(8,128)(2,1)S(1)}, u32[]{:S(2)}, u32[]{:S(2)}) collective-permute-start(bf16[512,256]{0,1:T(8,128)(2,1)S(1)} %collective-permute-done.2), channel_id=1, source_target_pairs={{0,1},{1,2},{2,3},{3,4},{4,5},{5,6},{6,7},{7,8},{8,9},{9,10},{10,1... | collective-permute-start | bytes 786440 | tf_op jit(solution)/shard_map/ppermute | solution.py:15
  158.4 7.0 %collective-permute-start.10 = (bf16[512,256]{0,1:T(8,128)(2,1)S(1)}, bf16[512,256]{0,1:T(8,128)(2,1)S(1)}, u32[]{:S(2)}, u32[]{:S(2)}) collective-permute-start(bf16[512,256]{0,1:T(8,128)(2,1)S(1)} %collective-permute-done.9), channel_id=1, source_target_pairs={{0,15},{1,0},{2,1},{3,2},{4,3},{5,4},{6,5},{7,6},{8,7},{9,8},{10,9... | collective-permute-start | bytes 786440 | tf_op jit(solution)/shard_map/ppermute | solution.py:17
  165.4 7.0 %collective-permute-start.4 = (bf16[512,256]{0,1:T(8,128)(2,1)S(1)}, bf16[512,256]{0,1:T(8,128)(2,1)S(1)}, u32[]{:S(2)}, u32[]{:S(2)}) collective-permute-start(bf16[512,256]{0,1:T(8,128)(2,1)S(1)} %collective-permute-done.3), channel_id=1, source_target_pairs={{0,1},{1,2},{2,3},{3,4},{4,5},{5,6},{6,7},{7,8},{8,9},{9,10},{10,1... | collective-permute-start | bytes 786440 | tf_op jit(solution)/shard_map/ppermute | solution.py:15
  165.4 7.2 %collective-permute-start.11 = (bf16[512,256]{0,1:T(8,128)(2,1)S(1)}, bf16[512,256]{0,1:T(8,128)(2,1)S(1)}, u32[]{:S(2)}, u32[]{:S(2)}) collective-permute-start(bf16[512,256]{0,1:T(8,128)(2,1)S(1)} %collective-permute-done.10), channel_id=1, source_target_pairs={{0,15},{1,0},{2,1},{3,2},{4,3},{5,4},{6,5},{7,6},{8,7},{9,8},{10,9... | collective-permute-start | bytes 786440 | tf_op jit(solution)/shard_map/ppermute | solution.py:17
  172.4 7.0 %collective-permute-start.5 = (bf16[512,256]{0,1:T(8,128)(2,1)S(1)}, bf16[512,256]{0,1:T(8,128)(2,1)S(1)}, u32[]{:S(2)}, u32[]{:S(2)}) collective-permute-start(bf16[512,256]{0,1:T(8,128)(2,1)S(1)} %collective-permute-done.4), channel_id=1, source_target_pairs={{0,1},{1,2},{2,3},{3,4},{4,5},{5,6},{6,7},{7,8},{8,9},{9,10},{10,1... | collective-permute-start | bytes 786440 | tf_op jit(solution)/shard_map/ppermute | solution.py:15
  172.6 7.4 %collective-permute-start.12 = (bf16[512,256]{0,1:T(8,128)(2,1)S(1)}, bf16[512,256]{0,1:T(8,128)(2,1)S(1)}, u32[]{:S(2)}, u32[]{:S(2)}) collective-permute-start(bf16[512,256]{0,1:T(8,128)(2,1)S(1)} %collective-permute-done.11), channel_id=1, source_target_pairs={{0,15},{1,0},{2,1},{3,2},{4,3},{5,4},{6,5},{7,6},{8,7},{9,8},{10,9... | collective-permute-start | bytes 786440 | tf_op jit(solution)/shard_map/ppermute | solution.py:17
  179.4 7.1 %collective-permute-start.6 = (bf16[512,256]{0,1:T(8,128)(2,1)S(1)}, bf16[512,256]{0,1:T(8,128)(2,1)}, u32[]{:S(2)}, u32[]{:S(2)}) collective-permute-start(bf16[512,256]{0,1:T(8,128)(2,1)S(1)} %collective-permute-done.5), channel_id=1, source_target_pairs={{0,1},{1,2},{2,3},{3,4},{4,5},{5,6},{6,7},{7,8},{8,9},{9,10},{10,1... | collective-permute-start | bytes 786440 | tf_op jit(solution)/shard_map/ppermute | solution.py:15
  180.0 7.0 %collective-permute-start.13 = (bf16[512,256]{0,1:T(8,128)(2,1)S(1)}, bf16[512,256]{0,1:T(8,128)(2,1)S(1)}, u32[]{:S(2)}, u32[]{:S(2)}) collective-permute-start(bf16[512,256]{0,1:T(8,128)(2,1)S(1)} %collective-permute-done.12), channel_id=1, source_target_pairs={{0,15},{1,0},{2,1},{3,2},{4,3},{5,4},{6,5},{7,6},{8,7},{9,8},{10,9... | collective-permute-start | bytes 786440 | tf_op jit(solution)/shard_map/ppermute | solution.py:17
  186.5 7.3 %collective-permute-start.7 = (bf16[512,256]{0,1:T(8,128)(2,1)}, bf16[512,256]{0,1:T(8,128)(2,1)}, u32[]{:S(2)}, u32[]{:S(2)}) collective-permute-start(bf16[512,256]{0,1:T(8,128)(2,1)} %collective-permute-done.6), channel_id=1, source_target_pairs={{0,1},{1,2},{2,3},{3,4},{4,5},{5,6},{6,7},{7,8},{8,9},{9,10},{10,1... | collective-permute-start | bytes 786440 | tf_op jit(solution)/shard_map/ppermute | solution.py:15
  187.0 19.5 %collective-permute-start.14 = (bf16[512,256]{0,1:T(8,128)(2,1)S(1)}, bf16[512,256]{0,1:T(8,128)(2,1)S(1)}, u32[]{:S(2)}, u32[]{:S(2)}) collective-permute-start(bf16[512,256]{0,1:T(8,128)(2,1)S(1)} %collective-permute-done.13), channel_id=1, source_target_pairs={{0,15},{1,0},{2,1},{3,2},{4,3},{5,4},{6,5},{7,6},{8,7},{9,8},{10,9... | collective-permute-start | bytes 786440 | tf_op jit(solution)/shard_map/ppermute | solution.py:17
Sparse Core Ops, SparseCore 0:
  11.9 87.2 all-gather.6
  102.3 83.9 all-gather.4
